TPU v7x, 32 devices: a whole 2x2x4 slice. The times are simulated.
32 devices in a mesh: fields: 2 (over x), prow: 8 (over z, y), pcol: 2 (over core).
Axes of the slice: x: 2, y: 2, z: 4, core: 2. Of those that a mesh axis runs over, the one named last changes fastest.
Arguments:
- inverse_tiles: bfloat16 [32, 16, 256, 256], P(('fields', 'prow'), 'pcol'), parts along dimension 0, may hold values from -6 to 6
- panel_blocks: bfloat16 [4, 8, 256, 512], P('fields', 'prow', None, 'pcol'), parts along dimension 0, may hold values from -0.125 to 0.125
- diag_inverse: float32 [4, 512], P('fields', 'pcol'), parts along dimension 0, may hold values from 0.5 to 2
- structure: int32 [4, 8], P('fields'), parts along dimension 0, may hold values from 0 to 15, as said below
- block_slot: int32 [32], P('fields'), parts along dimension 0, may hold values from 0 to 15, each once
Outputs:
- sigma_new: bfloat16 [4, 16, 256, 512], P('fields', 'prow', None, 'pcol'), parts along dimension 0
- variances: float32 [4, 512], P('fields', 'pcol'), parts along dimension 0
There are 2 independent parts, one for each index of `fields`. A program takes and returns all parts, laid end to end along the dimension named above; each array names one. Nothing has to cross between parts.
Inputs may be any that keep to these rules, and one draw needn't show every extreme that they name: `structure`: each row lists 8 distinct row blocks in increasing order, and the last is always 16 - 1. `block_slot`: each slot is used by exactly one row block.
All inputs are finite; a program needn't handle non-finite values.
Results may differ from a plain program's by a relative error of at most 0.0006.
Values may be sent and summed in bfloat16 or wider, within the bound.
No kernel may reach another device: no remote copies, remote signals or barrier semaphores. Data moves between devices by JAX's collectives and lax.ppermute only.
A program may use at most 128 MiB of HBM per device.

v0:
```python
import jax
import jax.numpy as jnp
from jax import lax
from jax.sharding import PartitionSpec as P


def swapped(shard, axis, stride):
    return lax.ppermute(shard, axis, [(i, i ^ 1 << stride) for i in range(lax.axis_size(axis))])


def make_accumulate(selected, row_hits, piece):
    contrib = jnp.einsum("iskxy,skyw->sixw", selected, piece, preferred_element_type=jnp.float32)
    own_panel = jnp.einsum("sik,skxw->sixw", row_hits, piece, preferred_element_type=jnp.float32)
    return (contrib, own_panel)


def per_device(inverse_tiles, panel_blocks, diag_inverse, structure, block_slot):
    rows_here = inverse_tiles.shape[0]
    tile_size = inverse_tiles.shape[2]
    supernodes = panel_blocks.shape[0]
    positions = structure.shape[1]
    prow_index = lax.axis_index("prow")
    pcol_index = lax.axis_index("pcol")
    slot_of = block_slot[structure]
    own_rows = prow_index * rows_here + jnp.arange(rows_here, dtype=jnp.int32)
    row_match = slot_of[:, None, :] == own_rows[None, :, None]
    row_hits = row_match.astype(jnp.bfloat16)
    row_used = jnp.any(row_match, axis=2)
    partner = swapped(inverse_tiles, "pcol", 0)
    first_half = jnp.where(pcol_index == 0, inverse_tiles, partner)
    second_half = jnp.where(pcol_index == 0, partner, inverse_tiles)
    whole_rows = jnp.concatenate([first_half, second_half], axis=1)
    selected = jnp.take(whole_rows, slot_of.reshape(-1), axis=1)
    selected = selected.reshape(rows_here, supernodes, positions, tile_size, tile_size)
    summed, own_panel = make_accumulate(
        selected, row_hits, lax.all_gather(panel_blocks, "prow", axis=1, tiled=True)
    )
    sigma_rows = jnp.where(row_used[:, :, None, None], -summed, jnp.zeros((), jnp.float32))
    partial_value = jnp.sum(own_panel * sigma_rows, axis=(1, 2))
    correction = lax.psum(partial_value, "prow")
    variances = diag_inverse - correction
    return (sigma_rows.astype(jnp.bfloat16), variances)


def solution(mesh):
    in_specs = (
        P(("fields", "prow"), "pcol", None, None),
        P("fields", "prow", None, "pcol"),
        P("fields", "pcol"),
        P("fields", None),
        P("fields"),
    )
    out_specs = (P("fields", "prow", None, "pcol"), P("fields", "pcol"))
    return jax.shard_map(
        per_device, mesh=mesh, in_specs=in_specs, out_specs=out_specs, check_vma=False
    )
```

profile of v0, /device:TPU:0, one launch (start us, length us, event | category | flops | bytes accessed | tf_op | source)
XLA Modules:
  0.0 95.9 jit_solution(17099047433927221169)
XLA Ops:
  7.2 0.0 copy-start
  7.2 0.0 all-gather.2.cloned.1.call-start
  7.2 0.7 all-gather.2.cloned.1.call-update
  7.9 0.6 collective-permute-start
  8.5 0.7 compare_select_fusion.1
  9.2 0.1 reshape.53
  9.2 0.0 copy-done
  9.2 0.7 gather_fusion
  9.9 0.1 reshape.52
  10.0 0.2 compare_reduce_fusion
  10.2 2.3 %collective-permute-done = bf16[2,8,256,256]{3,2,1,0:T(8,128)(2,1)S(1)} collective-permute-done((bf16[2,8,256,256]{3,2,1,0:T(8,128)(2,1)}, bf16[2,8,256,256]{3,2,1,0:T(8,128)(2,1)S(1)}, u32[]{:S(2)}, u32[]{:S(2)}) %collective-permute-start) | collective-permute-done | bytes 2097184 | tf_op jit(solution)/shard_map/ppermute | solution.py:8
  12.5 1.9 %broadcast_select_fusion.1 = (bf16[2,8,256,256]{3,2,1,0:T(8,128)(2,1)S(1)}, bf16[2,8,256,256]{3,2,1,0:T(8,128)(2,1)S(1)}) fusion(bf16[2,8,256,256]{3,2,1,0:T(8,128)(2,1)} %param.5, bf16[2,8,256,256]{3,2,1,0:T(8,128)(2,1)S(1)} %collective-permute-done, pred[]{:T(512)S(6)} %eq.20), kind=kLoop, calls=%fused_computation.11 | loop fusion | flops 2097152 | bytes 8388609 | tf_op jit(solution)/shard_map/jit(_where)/select_n | solution.py:30
  14.3 2.3 %pad_maximum_fusion = bf16[2,16,256,256]{3,2,1,0:T(8,128)(2,1)} fusion(bf16[2,8,256,256]{3,2,1,0:T(8,128)(2,1)S(1)} %get-tuple-element.3, bf16[2,8,256,256]{3,2,1,0:T(8,128)(2,1)S(1)} %get-tuple-element.2), kind=kLoop, calls=%fused_computation.2 | loop fusion | flops 2097152 | bytes 8388608 | tf_op jit(solution)/shard_map/concatenate | solution.py:32
  16.7 4.9 %gather_fusion.1 = bf16[16,2,256,256]{3,2,1,0:T(8,128)(2,1)} fusion(bf16[2,16,256,256]{3,2,1,0:T(8,128)(2,1)} %pad_maximum_fusion, s32[1024]{0:T(1024)S(1)} %pad_clamp_fusion), kind=kCustom, calls=%fused_computation.1 | custom fusion | bytes 8388672 | tf_op jit(solution)/shard_map/jit(_take)/gather | solution.py:33
  21.6 40.4 %all-gather.2.cloned.1.call-done = bf16[2,8,256,256]{3,2,1,0:T(8,128)(2,1)} async-done(((bf16[2,1,256,256]{3,2,1,0:T(8,128)(2,1)}), bf16[2,8,256,256]{3,2,1,0:T(8,128)(2,1)}) %all-gather.2.cloned.1.call-update) | async-done | bytes 2097168 | tf_op jit(solution)/shard_map/all_gather | solution.py:36
  62.0 0.0 copy-start.1
  62.0 3.2 %fusion.3 = f32[2,2,256,256]{3,1,2,0:T(2,128)S(1)} fusion(bf16[2,8,256,256]{3,2,1,0:T(8,128)(2,1)} %all-gather.2.cloned.1.call-done, s32[2,8]{1,0:T(2,128)S(1)} %reshape.52, s32[2]{0:T(128)S(1)} %iota_add_fusion), kind=kOutput, calls=%fused_computation.7 | convolution fusion | flops 4194336 | bytes 3145800 | tf_op jit(solution)/shard_map/sik,skxw->sixw/dot_general | solution.py:13
  65.2 0.0 copy-done.1
  65.2 0.0 copy-start.2
  65.2 4.3 %fusion.15 = (f32[2,256]{1,0:T(2,128)S(1)}, bf16[2,2,256,256]{3,2,1,0:T(8,128)(2,1)}) fusion(f32[2,2,256,256]{3,1,2,0:T(2,128)S(1)} %fusion.3, bf16[2,8,256,256]{3,2,1,0:T(8,128)(2,1)S(1)} %copy-done.1, bf16[2,2,8,256,256]{4,3,0,2,1:T(8,128)(2,1)} %bitcast.32, pred[2,8]{1,0:T(4,128)(4,1)S(1)} %compare_and_fusion, pred[2,2]{1,0:T(4,128)(4,1)S(1)} %compare_reduce_fusion), kind=kOutput, calls=%fused_computation.16 | convolution fusion | flops 1077149184 | bytes 7866388 | tf_op jit(solution)/shard_map/iskxy,skyw->sixw/dot_general | solution.py:12
  69.5 19.0 %psum.7 = f32[2,256]{1,0:T(2,128)S(1)} all-reduce(f32[2,256]{1,0:T(2,128)S(1)} %get-tuple-element.4), channel_id=1, replica_groups=mesh['fields'=2,'prow'=8,'pcol'=2] {'prow'}, use_global_device_ids=true, to_apply=%region_2.3 | all-reduce | flops 512 | bytes 4096 | tf_op jit(solution)/shard_map/psum | solution.py:40
  88.5 0.0 copy-done.2
  88.5 0.6 sub.3
  (5 shorter events, 0.0 us)
Async XLA Ops:
  7.2 2.1 %copy-start = (s32[16]{0:T(128)S(1)}, s32[16]{0:T(128)}, u32[]{:S(2)}) copy-start(s32[16]{0:T(128)} %param.9) | copy-start | bytes 196
  7.2 54.8 %all-gather.2.cloned.1.call-start = ((), (), s32[]{:S(2)}) async-start(), calls=%async_computation | async-start | bytes 2359296 | tf_op jit(solution)/shard_map/all_gather | solution.py:36
  7.9 4.6 %collective-permute-start = (bf16[2,8,256,256]{3,2,1,0:T(8,128)(2,1)}, bf16[2,8,256,256]{3,2,1,0:T(8,128)(2,1)S(1)}, u32[]{:S(2)}, u32[]{:S(2)}) collective-permute-start(bf16[2,8,256,256]{3,2,1,0:T(8,128)(2,1)} %param.5), channel_id=1, source_target_pairs={{0,1},{1,0},{2,3},{3,2},{4,5},{5,4},{6,7},{7,6},{8,9},{9,8},{10,11... | collective-permute-start | bytes 6291464 | tf_op jit(solution)/shard_map/ppermute | solution.py:8
  62.0 3.2 %copy-start.1 = (bf16[2,8,256,256]{3,2,1,0:T(8,128)(2,1)S(1)}, bf16[2,8,256,256]{3,2,1,0:T(8,128)(2,1)}, u32[]{:S(2)}) copy-start(bf16[2,8,256,256]{3,2,1,0:T(8,128)(2,1)} %all-gather.2.cloned.1.call-done) | copy-start | bytes 6291460
  65.2 23.3 %copy-start.2 = (f32[2,256]{1,0:T(2,128)S(1)}, f32[2,256]{1,0:T(2,128)}, u32[]{:S(2)}) copy-start(f32[2,256]{1,0:T(2,128)} %param.7) | copy-start | bytes 6148
Sparse Core Ops, SparseCore 0:
  10.2 51.7 all-gather.1
where the time goes:
time: 96.1 us; the launch traced here: 95.9 us
  waiting for transfers between devices  43.3 us (45%)
  blocking collectives  19 us (20%)
  between operations  14.1 us (15%)
  matrix products  7.51 us (8%)
  local copies, waits for them, and re-layouts  5.78 us (6%)
  other arithmetic  5.67 us (6%)
    all_gather x1, waiting for transfers between devices, per_device(): lax.all_gather(panel_blocks, 'prow', axis=1, tiled=True)  40.4 us
    psum x1, blocking collectives, per_device(): correction = lax.psum(partial_value, 'prow')  19 us
    gather x1, local copies, waits for them, and re-layouts, per_device(): selected = jnp.take(whole_rows, slot_of.reshape(-1), axis=1)  4.94 us
    dot_general x1, matrix products, make_accumulate(): jnp.einsum('iskxy,skyw->sixw', selected, piece, preferred_element_type=jn...  4.32 us
    dot_general x1, matrix products, make_accumulate(): jnp.einsum('sik,skxw->sixw', row_hits, piece, preferred_element_type=jnp....  3.19 us
    concatenate x1, other arithmetic, per_device(): whole_rows = jnp.concatenate([first_half, second_half], axis=1)  2.33 us
    ppermute x1, waiting for transfers between devices, swapped(): lax.ppermute(shard, axis, [(i, i ^ 1 << stride) for i in range(lax.axis_s...  2.26 us
  transfers between devices with their start and end apart: 2, of which 2 were waited for; matrix products, arithmetic and copies ran while one was open for 11% of the time, Pallas kernels for 0%

commit v1 on v0

--- a/solution.py
+++ b/solution.py
@@ -2,6 +2,11 @@
 import jax.numpy as jnp
 from jax import lax
 from jax.sharding import PartitionSpec as P
+
+
+def pack_lanes(incoming_x, ax_name):
+    part_now = jnp.sum(lax.all_gather(incoming_x, axis_name=ax_name), axis=0)
+    return part_now
 
 
 def swapped(shard, axis, stride):
@@ -37,7 +42,7 @@
     )
     sigma_rows = jnp.where(row_used[:, :, None, None], -summed, jnp.zeros((), jnp.float32))
     partial_value = jnp.sum(own_panel * sigma_rows, axis=(1, 2))
-    correction = lax.psum(partial_value, "prow")
+    correction = pack_lanes(partial_value, "prow")
     variances = diag_inverse - correction
     return (sigma_rows.astype(jnp.bfloat16), variances)
 

time: 96.1 us -> 103 us (1.072)
  blocking collectives: 19 us -> 26.1 us
    all_gather x0 -> x1, blocking collectives: none -> 26.1 us  [pack_lanes(): part_now = jnp.sum(lax.all_gather(incoming_x, axis_name=ax_name), axis=0)]
    psum x1 -> x0, blocking collectives: 19 us -> none  [per_device(): correction = lax.psum(partial_value, 'prow')]
where the time goes in v1:
time: 103 us
  waiting for transfers between devices  43.3 us (42%)
  blocking collectives  26.1 us (25%)
  between operations  14.1 us (14%)
  matrix products  7.51 us (7%)
  local copies, waits for them, and re-layouts  5.78 us (6%)
  other arithmetic  5.69 us (6%)
    all_gather x1, waiting for transfers between devices, per_device(): lax.all_gather(panel_blocks, 'prow', axis=1, tiled=True)  40.4 us
    all_gather x1, blocking collectives, pack_lanes(): part_now = jnp.sum(lax.all_gather(incoming_x, axis_name=ax_name), axis=0)  26.1 us
    gather x1, local copies, waits for them, and re-layouts, per_device(): selected = jnp.take(whole_rows, slot_of.reshape(-1), axis=1)  4.94 us
    dot_general x1, matrix products, make_accumulate(): jnp.einsum('iskxy,skyw->sixw', selected, piece, preferred_element_type=jn...  4.32 us
    dot_general x1, matrix products, make_accumulate(): jnp.einsum('sik,skxw->sixw', row_hits, piece, preferred_element_type=jnp....  3.19 us
    concatenate x1, other arithmetic, per_device(): whole_rows = jnp.concatenate([first_half, second_half], axis=1)  2.33 us
    ppermute x1, waiting for transfers between devices, swapped(): lax.ppermute(shard, axis, [(i, i ^ 1 << stride) for i in range(lax.axis_s...  2.26 us
  transfers between devices with their start and end apart: 2, of which 2 were waited for; matrix products, arithmetic and copies ran while one was open for 11% of the time, Pallas kernels for 0%

profile of v1, /device:TPU:0, one launch (start us, length us, event | category | flops | bytes accessed | tf_op | source)
XLA Modules:
  0.0 103.1 jit_solution(17944252983502595990)
XLA Ops:
  7.2 0.0 copy-start
  7.2 0.0 all-gather.4.cloned.1.call-start
  7.2 0.7 all-gather.4.cloned.1.call-update
  7.9 0.6 collective-permute-start
  8.5 0.7 compare_select_fusion.1
  9.2 0.1 reshape.53
  9.2 0.0 copy-done
  9.2 0.7 gather_fusion
  9.9 0.1 reshape.52
  10.0 0.2 compare_reduce_fusion
  10.2 2.3 %collective-permute-done = bf16[2,8,256,256]{3,2,1,0:T(8,128)(2,1)S(1)} collective-permute-done((bf16[2,8,256,256]{3,2,1,0:T(8,128)(2,1)}, bf16[2,8,256,256]{3,2,1,0:T(8,128)(2,1)S(1)}, u32[]{:S(2)}, u32[]{:S(2)}) %collective-permute-start) | collective-permute-done | bytes 2097184 | tf_op jit(solution)/shard_map/ppermute | solution.py:13
  12.5 1.9 %broadcast_select_fusion.1 = (bf16[2,8,256,256]{3,2,1,0:T(8,128)(2,1)S(1)}, bf16[2,8,256,256]{3,2,1,0:T(8,128)(2,1)S(1)}) fusion(bf16[2,8,256,256]{3,2,1,0:T(8,128)(2,1)} %param.5, bf16[2,8,256,256]{3,2,1,0:T(8,128)(2,1)S(1)} %collective-permute-done, pred[]{:T(512)S(6)} %eq.20), kind=kLoop, calls=%fused_computation.11 | loop fusion | flops 2097152 | bytes 8388609 | tf_op jit(solution)/shard_map/jit(_where)/select_n | solution.py:35
  14.3 2.3 %pad_maximum_fusion = bf16[2,16,256,256]{3,2,1,0:T(8,128)(2,1)} fusion(bf16[2,8,256,256]{3,2,1,0:T(8,128)(2,1)S(1)} %get-tuple-element.3, bf16[2,8,256,256]{3,2,1,0:T(8,128)(2,1)S(1)} %get-tuple-element.2), kind=kLoop, calls=%fused_computation.2 | loop fusion | flops 2097152 | bytes 8388608 | tf_op jit(solution)/shard_map/concatenate | solution.py:37
  16.7 4.9 %gather_fusion.1 = bf16[16,2,256,256]{3,2,1,0:T(8,128)(2,1)} fusion(bf16[2,16,256,256]{3,2,1,0:T(8,128)(2,1)} %pad_maximum_fusion, s32[1024]{0:T(1024)S(1)} %pad_clamp_fusion), kind=kCustom, calls=%fused_computation.1 | custom fusion | bytes 8388672 | tf_op jit(solution)/shard_map/jit(_take)/gather | solution.py:38
  21.6 40.4 %all-gather.4.cloned.1.call-done = bf16[2,8,256,256]{3,2,1,0:T(8,128)(2,1)} async-done(((bf16[2,1,256,256]{3,2,1,0:T(8,128)(2,1)}), bf16[2,8,256,256]{3,2,1,0:T(8,128)(2,1)}) %all-gather.4.cloned.1.call-update) | async-done | bytes 2097168 | tf_op jit(solution)/shard_map/all_gather | solution.py:41
  62.0 0.0 copy-start.1
  62.0 3.2 %fusion.3 = f32[2,2,256,256]{3,1,2,0:T(2,128)S(1)} fusion(bf16[2,8,256,256]{3,2,1,0:T(8,128)(2,1)} %all-gather.4.cloned.1.call-done, s32[2,8]{1,0:T(2,128)S(1)} %reshape.52, s32[2]{0:T(128)S(1)} %iota_add_fusion), kind=kOutput, calls=%fused_computation.7 | convolution fusion | flops 4194336 | bytes 3145800 | tf_op jit(solution)/shard_map/sik,skxw->sixw/dot_general | solution.py:18
  65.2 0.0 copy-done.1
  65.2 0.0 copy-start.2
  65.2 4.3 %fusion.15 = (f32[2,256]{1,0:T(2,128)S(1)}, bf16[2,2,256,256]{3,2,1,0:T(8,128)(2,1)}) fusion(f32[2,2,256,256]{3,1,2,0:T(2,128)S(1)} %fusion.3, bf16[2,8,256,256]{3,2,1,0:T(8,128)(2,1)S(1)} %copy-done.1, bf16[2,2,8,256,256]{4,3,0,2,1:T(8,128)(2,1)} %bitcast.33, pred[2,8]{1,0:T(4,128)(4,1)S(1)} %compare_and_fusion, pred[2,2]{1,0:T(4,128)(4,1)S(1)} %compare_reduce_fusion), kind=kOutput, calls=%fused_computation.16 | convolution fusion | flops 1077149184 | bytes 7866388 | tf_op jit(solution)/shard_map/iskxy,skyw->sixw/dot_general | solution.py:17
  69.5 26.1 %all-gather.1 = f32[8,2,256]{2,1,0:T(2,128)S(1)} all-gather(f32[1,2,256]{2,1,0:T(2,128)S(1)} %bitcast.34), channel_id=2, replica_groups=mesh['fields'=2,'prow'=8,'pcol'=2] {'prow'}, dimensions={0}, use_global_device_ids=true | all-gather | bytes 18432 | tf_op jit(solution)/shard_map/all_gather | solution.py:8
  95.6 0.0 copy-done.2
  95.7 0.6 sub.3
  (6 shorter events, 0.1 us)
Async XLA Ops:
  7.2 2.1 %copy-start = (s32[16]{0:T(128)S(1)}, s32[16]{0:T(128)}, u32[]{:S(2)}) copy-start(s32[16]{0:T(128)} %param.9) | copy-start | bytes 196
  7.2 54.8 %all-gather.4.cloned.1.call-start = ((), (), s32[]{:S(2)}) async-start(), calls=%async_computation | async-start | bytes 2359296 | tf_op jit(solution)/shard_map/all_gather | solution.py:41
  7.9 4.6 %collective-permute-start = (bf16[2,8,256,256]{3,2,1,0:T(8,128)(2,1)}, bf16[2,8,256,256]{3,2,1,0:T(8,128)(2,1)S(1)}, u32[]{:S(2)}, u32[]{:S(2)}) collective-permute-start(bf16[2,8,256,256]{3,2,1,0:T(8,128)(2,1)} %param.5), channel_id=1, source_target_pairs={{0,1},{1,0},{2,3},{3,2},{4,5},{5,4},{6,7},{7,6},{8,9},{9,8},{10,11... | collective-permute-start | bytes 6291464 | tf_op jit(solution)/shard_map/ppermute | solution.py:13
  62.0 3.2 %copy-start.1 = (bf16[2,8,256,256]{3,2,1,0:T(8,128)(2,1)S(1)}, bf16[2,8,256,256]{3,2,1,0:T(8,128)(2,1)}, u32[]{:S(2)}) copy-start(bf16[2,8,256,256]{3,2,1,0:T(8,128)(2,1)} %all-gather.4.cloned.1.call-done) | copy-start | bytes 6291460
  65.2 30.5 %copy-start.2 = (f32[2,256]{1,0:T(2,128)S(1)}, f32[2,256]{1,0:T(2,128)}, u32[]{:S(2)}) copy-start(f32[2,256]{1,0:T(2,128)} %param.7) | copy-start | bytes 6148
Sparse Core Ops, SparseCore 0:
  10.2 51.7 all-gather.3
